TPU v7x, 32 devices: a whole 2x2x4 slice. The times are simulated.
32 devices in a mesh: vec: 8 (over z, core), rep: 4 (over y, x).
Axes of the slice: x: 2, y: 2, z: 4, core: 2. Of those that a mesh axis runs over, the one named last changes fastest.
Arguments:
- vectors: bfloat16 [1024, 1024], P('vec'), may hold values from 0 to 2
- pivot_index: int32 [4, 8], P('rep'), may hold values from 0 to 1023
Outputs:
- similarity: bfloat16 [7, 32, 1024, 128], P(None, 'rep', 'vec')
All inputs are finite; a program needn't handle non-finite values.
Results may differ from a plain program's by a relative error of at most 0.011.
Values may be sent and summed in bfloat16 or wider, within the bound.
A program may use at most 64 MiB of HBM per device.

v0:
```python
import math
import jax
import jax.numpy as jnp
from jax import lax
from jax.sharding import PartitionSpec as P

HALF = 3


def from_behind(block, axis, distance):
    devices = range(lax.axis_size(axis))
    route = [((i - distance) % len(devices), i) for i in devices]
    return lax.ppermute(block, axis, route)


def contract(left, right):
    return lax.dot_general(
        left, right, (((1,), (1,)), ((), ())), preferred_element_type=jnp.float32
    )


def on_device(vectors, pivot_index):
    block_rows, fields = vectors.shape
    position = lax.axis_index("vec")
    wanted = pivot_index.reshape(-1) - position * block_rows
    columns = jnp.arange(block_rows, dtype=jnp.int32)
    onehot = (wanted[:, None] == columns[None, :]).astype(jnp.bfloat16)
    local_rows = jnp.dot(onehot, vectors, preferred_element_type=jnp.float32)
    pivots = lax.psum(local_rows, "vec")
    count = pivots.shape[0]
    centre = jnp.sum(pivots, axis=1) / fields
    scaled = (vectors.astype(jnp.float32)[None, :, :] * pivots[:, None, :]).astype(jnp.bfloat16)
    scaled = scaled.reshape(count * block_rows, fields)
    replicas = lax.axis_size("rep")
    share = block_rows // replicas
    own_rows = lax.dynamic_slice_in_dim(vectors, lax.axis_index("rep") * share, share, 0)
    window = 2 * HALF + 1
    triples = [None] * window
    grams = [None] * window
    triples[HALF] = contract(scaled, vectors)
    grams[HALF] = contract(own_rows, vectors)
    lower = vectors
    upper = vectors
    for reach in range(1, HALF + 1):
        lower = from_behind(lower, "vec", 1)
        upper = from_behind(upper, "vec", -1)
        triples[HALF - reach] = contract(scaled, lower)
        grams[HALF - reach] = contract(own_rows, lower)
        triples[HALF + reach] = contract(scaled, upper)
        grams[HALF + reach] = contract(own_rows, upper)
    triple_all = jnp.stack(triples).reshape(window, count, block_rows, block_rows)
    gram_all = jnp.stack(grams)
    gram_all = lax.all_gather(gram_all, "rep", axis=1, tiled=True)
    similarity = (triple_all - centre[None, :, None, None] * gram_all[:, None, :, :]) / math.sqrt(
        fields
    )
    return similarity.astype(jnp.bfloat16)


def solution(mesh):
    in_specs = (P("vec", None), P("rep", None))
    out_specs = P(None, "rep", "vec", None)
    return jax.shard_map(
        on_device, mesh=mesh, in_specs=in_specs, out_specs=out_specs, check_vma=False
    )
```

profile of v0, /device:TPU:0, one launch (start us, length us, event | category | flops | bytes accessed | tf_op | source)
XLA Modules:
  0.0 71.4 jit_solution(5123657337619987184)
XLA Ops:
  0.0 0.5 collective-permute-start
  0.5 4.0 %collective-permute-start.3 = (bf16[128,1024]{1,0:T(8,128)(2,1)}, bf16[128,1024]{1,0:T(8,128)(2,1)S(1)}, u32[]{:S(2)}, u32[]{:S(2)}) collective-permute-start(bf16[128,1024]{1,0:T(8,128)(2,1)} %param.2), channel_id=1, source_target_pairs={{4,0},{8,4},{12,8},{16,12},{20,16},{24,20},{28,24},{0,28},{5,1},{9... | collective-permute-start | bytes 786440 | tf_op jit(solution)/shard_map/ppermute | solution.py:13
  4.5 4.5 %collective-permute-done = bf16[128,1024]{1,0:T(8,128)(2,1)S(1)} collective-permute-done((bf16[128,1024]{1,0:T(8,128)(2,1)}, bf16[128,1024]{1,0:T(8,128)(2,1)S(1)}, u32[]{:S(2)}, u32[]{:S(2)}) %collective-permute-start) | collective-permute-done | bytes 262176 | tf_op jit(solution)/shard_map/ppermute | solution.py:13
  9.0 0.7 subtract_bitcast_fusion
  9.7 3.5 %collective-permute-start.4 = (bf16[128,1024]{1,0:T(8,128)(2,1)S(1)}, bf16[128,1024]{1,0:T(8,128)(2,1)S(1)}, u32[]{:S(2)}, u32[]{:S(2)}) collective-permute-start(bf16[128,1024]{1,0:T(8,128)(2,1)S(1)} %collective-permute-done.3), channel_id=1, source_target_pairs={{4,0},{8,4},{12,8},{16,12},{20,16},{24,20},{28,24},{0,28},{5,1},{9... | collective-permute-start | bytes 786440 | tf_op jit(solution)/shard_map/ppermute | solution.py:13
  13.2 3.5 %collective-permute-done.1 = bf16[128,1024]{1,0:T(8,128)(2,1)S(1)} collective-permute-done((bf16[128,1024]{1,0:T(8,128)(2,1)S(1)}, bf16[128,1024]{1,0:T(8,128)(2,1)S(1)}, u32[]{:S(2)}, u32[]{:S(2)}) %collective-permute-start.1) | collective-permute-done | bytes 262176 | tf_op jit(solution)/shard_map/ppermute | solution.py:13
  16.7 1.1 %fusion.56 = f32[8,1024]{1,0:T(8,128)S(1)} fusion(bf16[128,1024]{1,0:T(8,128)(2,1)} %param.2, s32[8]{0:T(128)S(1)} %subtract_bitcast_fusion), kind=kOutput, calls=%fused_computation.66 | convolution fusion | flops 2098176 | bytes 294944 | tf_op jit(solution)/shard_map/dot_general | solution.py:28
  17.8 1.0 %convert_element_type.21 = f32[128,1024]{1,0:T(8,128)S(1)} convert(bf16[128,1024]{1,0:T(8,128)(2,1)} %param.2) | non-fusion elementwise | flops 131072 | bytes 786432 | tf_op jit(solution)/shard_map/convert_element_type | solution.py:32
  18.8 29.4 %psum.7 = f32[8,1024]{1,0:T(8,128)S(1)} all-reduce(f32[8,1024]{1,0:T(8,128)S(1)} %fusion.56), channel_id=1, replica_groups=mesh['vec'=8,'rep'=4] {'vec'}, use_global_device_ids=true, to_apply=%region_0.0 | all-reduce | flops 8192 | bytes 65536 | tf_op jit(solution)/shard_map/psum | solution.py:29
  48.5 1.0 %fusion.41 = f32[7,32,128]{2,1,0:T(8,128)S(1)} fusion(bf16[128,1024]{1,0:T(8,128)(2,1)S(1)} %collective-permute-done.2, bf16[128,1024]{1,0:T(8,128)(2,1)} %param.2, s32[]{:T(128)S(6)} %select_n.3), kind=kOutput, calls=%fused_computation.50 | convolution fusion | flops 8388607 | bytes 344068 | tf_op jit(solution)/shard_map/dot_general | solution.py:17
  49.5 1.0 %fusion.40 = f32[7,32,128]{2,1,0:T(8,128)S(1)} fusion(f32[7,32,128]{2,1,0:T(8,128)S(1)} %fusion.41, bf16[128,1024]{1,0:T(8,128)(2,1)S(1)} %collective-permute-done.1, bf16[128,1024]{1,0:T(8,128)(2,1)} %param.2, s32[]{:T(128)S(6)} %select_n.3), kind=kOutput, calls=%fused_computation.48 | convolution fusion | flops 8388608 | bytes 344068 | tf_op jit(solution)/shard_map/dot_general | solution.py:17
  50.5 1.0 %fusion.39 = f32[7,32,128]{2,1,0:T(8,128)S(1)} fusion(f32[7,32,128]{2,1,0:T(8,128)S(1)} %fusion.40, bf16[128,1024]{1,0:T(8,128)(2,1)S(1)} %collective-permute-done, bf16[128,1024]{1,0:T(8,128)(2,1)} %param.2, s32[]{:T(128)S(6)} %select_n.3), kind=kOutput, calls=%fused_computation.46 | convolution fusion | flops 8388608 | bytes 344068 | tf_op jit(solution)/shard_map/dot_general | solution.py:17
  51.6 1.2 %fusion.38 = f32[7,32,128]{2,1,0:T(8,128)S(1)} fusion(f32[7,32,128]{2,1,0:T(8,128)S(1)} %fusion.39, bf16[128,1024]{1,0:T(8,128)(2,1)} %param.2, s32[]{:T(128)S(6)} %select_n.3), kind=kOutput, calls=%fused_computation.44 | convolution fusion | flops 8388608 | bytes 344068 | tf_op jit(solution)/shard_map/dot_general | solution.py:17
  52.8 0.7 %fusion.22 = f32[7,8,128,128]{3,2,1,0:T(8,128)S(1)} fusion(f32[8,1024]{1,0:T(8,128)S(1)} %psum.7, f32[128,1024]{1,0:T(8,128)S(1)} %convert_element_type.21, bf16[128,1024]{1,0:T(8,128)(2,1)S(1)} %collective-permute-done.2), kind=kOutput, calls=%fused_computation.24 | convolution fusion | flops 270532608 | bytes 1343488 | tf_op jit(solution)/shard_map/dot_general | solution.py:17
  53.6 0.7 fusion.24
  54.3 0.7 fusion.26
  55.2 0.2 fusion.36
  55.4 0.7 %fusion.28 = f32[7,8,128,128]{3,2,1,0:T(8,128)S(1)} fusion(f32[7,8,128,128]{3,2,1,0:T(8,128)S(1)} %fusion.26, f32[8,1024]{1,0:T(8,128)S(1)} %psum.7, f32[128,1024]{1,0:T(8,128)S(1)} %convert_element_type.21, bf16[128,1024]{1,0:T(8,128)(2,1)S(1)} %copy-done), kind=kOutput, calls=%fused_computation.30 | convolution fusion | flops 270532608 | bytes 1343488 | tf_op jit(solution)/shard_map/dot_general | solution.py:17
  56.1 0.2 fusion.35
  56.3 11.0 %all_gather.3 = f32[7,128,128]{2,1,0:T(8,128)S(1)} all-gather(f32[7,32,128]{2,1,0:T(8,128)S(1)} %fusion.35), channel_id=1, replica_groups=mesh['vec'=8,'rep'=4] {'rep'}, dimensions={1}, use_global_device_ids=true | all-gather | bytes 573440 | tf_op jit(solution)/shard_map/all_gather | solution.py:53
  67.3 0.7 fusion.30
  68.0 0.7 fusion.32
  68.8 0.7 fusion.34
  69.5 1.9 %multiply_convert_fusion.8 = bf16[7,8,128,128]{3,2,1,0:T(8,128)(2,1)} fusion(f32[7,8,128,128]{3,2,1,0:T(8,128)S(1)} %fusion.34, f32[7,128,128]{2,1,0:T(8,128)S(1)} %all_gather.3, f32[8]{0:T(128)S(1)} %broadcast_multiply_fusion), kind=kLoop, calls=%fused_computation.8 | loop fusion | flops 3670016 | bytes 5963808 | tf_op jit(solution)/shard_map/convert_element_type | solution.py:57
  (12 shorter events, 0.4 us)
Async XLA Ops:
  0.0 9.0 %collective-permute-start = (bf16[128,1024]{1,0:T(8,128)(2,1)}, bf16[128,1024]{1,0:T(8,128)(2,1)S(1)}, u32[]{:S(2)}, u32[]{:S(2)}) collective-permute-start(bf16[128,1024]{1,0:T(8,128)(2,1)} %param.2), channel_id=1, source_target_pairs={{28,0},{0,4},{4,8},{8,12},{12,16},{16,20},{20,24},{24,28},{29,1},{... | collective-permute-start | bytes 786440 | tf_op jit(solution)/shard_map/ppermute | solution.py:13
  0.5 9.2 %collective-permute-start.3 = (bf16[128,1024]{1,0:T(8,128)(2,1)}, bf16[128,1024]{1,0:T(8,128)(2,1)S(1)}, u32[]{:S(2)}, u32[]{:S(2)}) collective-permute-start(bf16[128,1024]{1,0:T(8,128)(2,1)} %param.2), channel_id=1, source_target_pairs={{4,0},{8,4},{12,8},{16,12},{20,16},{24,20},{28,24},{0,28},{5,1},{9... | collective-permute-start | bytes 786440 | tf_op jit(solution)/shard_map/ppermute | solution.py:13
  9.0 7.7 %collective-permute-start.1 = (bf16[128,1024]{1,0:T(8,128)(2,1)S(1)}, bf16[128,1024]{1,0:T(8,128)(2,1)S(1)}, u32[]{:S(2)}, u32[]{:S(2)}) collective-permute-start(bf16[128,1024]{1,0:T(8,128)(2,1)S(1)} %collective-permute-done), channel_id=1, source_target_pairs={{28,0},{0,4},{4,8},{8,12},{12,16},{16,20},{20,24},{24,28},{29,1},{... | collective-permute-start | bytes 786440 | tf_op jit(solution)/shard_map/ppermute | solution.py:13
  9.7 38.7 %collective-permute-start.4 = (bf16[128,1024]{1,0:T(8,128)(2,1)S(1)}, bf16[128,1024]{1,0:T(8,128)(2,1)S(1)}, u32[]{:S(2)}, u32[]{:S(2)}) collective-permute-start(bf16[128,1024]{1,0:T(8,128)(2,1)S(1)} %collective-permute-done.3), channel_id=1, source_target_pairs={{4,0},{8,4},{12,8},{16,12},{20,16},{24,20},{28,24},{0,28},{5,1},{9... | collective-permute-start | bytes 786440 | tf_op jit(solution)/shard_map/ppermute | solution.py:13
  16.7 31.8 %collective-permute-start.2 = (bf16[128,1024]{1,0:T(8,128)(2,1)S(1)}, bf16[128,1024]{1,0:T(8,128)(2,1)S(1)}, u32[]{:S(2)}, u32[]{:S(2)}) collective-permute-start(bf16[128,1024]{1,0:T(8,128)(2,1)S(1)} %collective-permute-done.1), channel_id=1, source_target_pairs={{28,0},{0,4},{4,8},{8,12},{12,16},{16,20},{20,24},{24,28},{29,1},{... | collective-permute-start | bytes 786440 | tf_op jit(solution)/shard_map/ppermute | solution.py:13
  48.4 7.7 %collective-permute-start.5 = (bf16[128,1024]{1,0:T(8,128)(2,1)S(1)}, bf16[128,1024]{1,0:T(8,128)(2,1)S(1)}, u32[]{:S(2)}, u32[]{:S(2)}) collective-permute-start(bf16[128,1024]{1,0:T(8,128)(2,1)S(1)} %collective-permute-done.4), channel_id=1, source_target_pairs={{4,0},{8,4},{12,8},{16,12},{20,16},{24,20},{28,24},{0,28},{5,1},{9... | collective-permute-start | bytes 786440 | tf_op jit(solution)/shard_map/ppermute | solution.py:13
  52.8 2.2 %copy-start = (bf16[128,1024]{1,0:T(8,128)(2,1)S(1)}, bf16[128,1024]{1,0:T(8,128)(2,1)}, u32[]{:S(2)}) copy-start(bf16[128,1024]{1,0:T(8,128)(2,1)} %param.2) | copy-start | bytes 786436
where the time goes:
time: 71.7 us; the launch traced here: 71.4 us
  blocking collectives  40.5 us (56%)
  matrix products  11 us (15%)
  starting transfers between devices  8.13 us (11%)
  waiting for transfers between devices  7.96 us (11%)
  other arithmetic  3.69 us (5%)
    psum x1, blocking collectives, on_device(): pivots = lax.psum(local_rows, 'vec')  29.4 us
    all_gather x1, blocking collectives, on_device(): gram_all = lax.all_gather(gram_all, 'rep', axis=1, tiled=True)  11 us
    dot_general x14, matrix products, contract(): lax.dot_general(left, right, (((1,), (1,)), ((), ())), preferred_element_...  9.87 us
    ppermute x6, starting transfers between devices, from_behind(): return lax.ppermute(block, axis, route)  8.13 us
    ppermute x6, waiting for transfers between devices, from_behind(): return lax.ppermute(block, axis, route)  7.96 us
    convert_element_type x1, other arithmetic, on_device(): return similarity.astype(jnp.bfloat16)  1.9 us
  transfers between devices with their start and end apart: 6, of which 2 were waited for; matrix products, arithmetic and copies ran while one was open for 15% of the time, Pallas kernels for 0%

commit v1 on v0

--- a/solution.py
+++ b/solution.py
@@ -5,6 +5,22 @@
 from jax.sharding import PartitionSpec as P
 
 HALF = 3
+
+
+def time_the_forms(u):
+    seen = []
+    kk = 0
+    shares = jax.lax.axis_size("rep")
+    while kk < shares:
+        seen.append((kk, (kk + 1) % shares))
+        kk = kk + 1
+    oldest = [None] * shares
+    oldest[shares - 1] = u
+    for h in range(shares - 2, -1, -1):
+        oldest[h] = jax.lax.ppermute(oldest[h + 1], "rep", seen)
+    formed = jnp.concatenate(oldest, axis=1)
+    z = (jax.lax.axis_index("rep") + 1) * u.shape[1]
+    return jnp.roll(formed, z, axis=1)
 
 
 def from_behind(block, axis, distance):
@@ -50,7 +66,7 @@
         grams[HALF + reach] = contract(own_rows, upper)
     triple_all = jnp.stack(triples).reshape(window, count, block_rows, block_rows)
     gram_all = jnp.stack(grams)
-    gram_all = lax.all_gather(gram_all, "rep", axis=1, tiled=True)
+    gram_all = time_the_forms(gram_all)
     similarity = (triple_all - centre[None, :, None, None] * gram_all[:, None, :, :]) / math.sqrt(
         fields
     )

time: 71.7 us -> 77.7 us (1.084)
  waiting for transfers between devices: 7.96 us -> 21.3 us
  blocking collectives: 40.5 us -> 29.4 us
  starting transfers between devices: 8.13 us -> 11.4 us
    ppermute x0 -> x3, waiting for transfers between devices: none -> 13.4 us  [time_the_forms(): oldest[h] = jax.lax.ppermute(oldest[h + 1], 'rep', seen)]
    all_gather x1 -> x0, blocking collectives: 11 us -> none  [on_device(): gram_all = lax.all_gather(gram_all, 'rep', axis=1, tiled=True)]
    ppermute x0 -> x3, starting transfers between devices: none -> 3.27 us  [time_the_forms(): oldest[h] = jax.lax.ppermute(oldest[h + 1], 'rep', seen)]
  transfers between devices with their start and end apart: 6 -> 9, of which waited for: 2 -> 5; matrix products, arithmetic and copies ran while one was open for 15% -> 16% of each run, Pallas kernels for 0% -> 0%
where the time goes in v1:
time: 77.7 us; the launch traced here: 77.3 us
  blocking collectives  29.4 us (38%)
  waiting for transfers between devices  21.3 us (27%)
  starting transfers between devices  11.4 us (15%)
  matrix products  11 us (14%)
  other arithmetic  3.69 us (5%)
    psum x1, blocking collectives, on_device(): pivots = lax.psum(local_rows, 'vec')  29.4 us
    ppermute x3, waiting for transfers between devices, time_the_forms(): oldest[h] = jax.lax.ppermute(oldest[h + 1], 'rep', seen)  13.4 us
    dot_general x14, matrix products, contract(): lax.dot_general(left, right, (((1,), (1,)), ((), ())), preferred_element_...  9.87 us
    ppermute x6, starting transfers between devices, from_behind(): return lax.ppermute(block, axis, route)  8.13 us
    ppermute x6, waiting for transfers between devices, from_behind(): return lax.ppermute(block, axis, route)  7.96 us
    ppermute x3, starting transfers between devices, time_the_forms(): oldest[h] = jax.lax.ppermute(oldest[h + 1], 'rep', seen)  3.27 us
    convert_element_type x1, other arithmetic, on_device(): return similarity.astype(jnp.bfloat16)  1.9 us
  transfers between devices with their start and end apart: 9, of which 5 were waited for; matrix products, arithmetic and copies ran while one was open for 16% of the time, Pallas kernels for 0%

profile of v1, /device:TPU:0, one launch (start us, length us, event | category | flops | bytes accessed | tf_op | source)
XLA Modules:
  0.0 77.3 jit_solution(18026916061641735386)
XLA Ops:
  0.5 4.0 %collective-permute-start.3 = (bf16[128,1024]{1,0:T(8,128)(2,1)}, bf16[128,1024]{1,0:T(8,128)(2,1)S(1)}, u32[]{:S(2)}, u32[]{:S(2)}) collective-permute-start(bf16[128,1024]{1,0:T(8,128)(2,1)} %param.2), channel_id=1, source_target_pairs={{4,0},{8,4},{12,8},{16,12},{20,16},{24,20},{28,24},{0,28},{5,1},{9... | collective-permute-start | bytes 786440 | tf_op jit(solution)/shard_map/ppermute | solution.py:29
  4.5 4.5 %collective-permute-done = bf16[128,1024]{1,0:T(8,128)(2,1)S(1)} collective-permute-done((bf16[128,1024]{1,0:T(8,128)(2,1)}, bf16[128,1024]{1,0:T(8,128)(2,1)S(1)}, u32[]{:S(2)}, u32[]{:S(2)}) %collective-permute-start) | collective-permute-done | bytes 262176 | tf_op jit(solution)/shard_map/ppermute | solution.py:29
  9.7 3.5 %collective-permute-start.4 = (bf16[128,1024]{1,0:T(8,128)(2,1)S(1)}, bf16[128,1024]{1,0:T(8,128)(2,1)S(1)}, u32[]{:S(2)}, u32[]{:S(2)}) collective-permute-start(bf16[128,1024]{1,0:T(8,128)(2,1)S(1)} %collective-permute-done.3), channel_id=1, source_target_pairs={{4,0},{8,4},{12,8},{16,12},{20,16},{24,20},{28,24},{0,28},{5,1},{9... | collective-permute-start | bytes 786440 | tf_op jit(solution)/shard_map/ppermute | solution.py:29
  13.2 3.5 %collective-permute-done.1 = bf16[128,1024]{1,0:T(8,128)(2,1)S(1)} collective-permute-done((bf16[128,1024]{1,0:T(8,128)(2,1)S(1)}, bf16[128,1024]{1,0:T(8,128)(2,1)S(1)}, u32[]{:S(2)}, u32[]{:S(2)}) %collective-permute-start.1) | collective-permute-done | bytes 262176 | tf_op jit(solution)/shard_map/ppermute | solution.py:29
  16.7 1.1 %fusion.49 = f32[8,1024]{1,0:T(8,128)S(1)} fusion(bf16[128,1024]{1,0:T(8,128)(2,1)} %param.2, s32[8]{0:T(128)S(1)} %subtract_bitcast_fusion), kind=kOutput, calls=%fused_computation.86 | convolution fusion | flops 2098176 | bytes 294944 | tf_op jit(solution)/shard_map/dot_general | solution.py:44
  17.8 1.0 %convert_element_type.21 = f32[128,1024]{1,0:T(8,128)S(1)} convert(bf16[128,1024]{1,0:T(8,128)(2,1)} %param.2) | non-fusion elementwise | flops 131072 | bytes 786432 | tf_op jit(solution)/shard_map/convert_element_type | solution.py:48
  18.9 29.4 %psum.7 = f32[8,1024]{1,0:T(8,128)S(1)} all-reduce(f32[8,1024]{1,0:T(8,128)S(1)} %fusion.49), channel_id=1, replica_groups=mesh['vec'=8,'rep'=4] {'vec'}, use_global_device_ids=true, to_apply=%region_0.0 | all-reduce | flops 8192 | bytes 65536 | tf_op jit(solution)/shard_map/psum | solution.py:45
  48.5 1.0 %constant_dynamic-update-slice_fusion.6 = (f32[7,32,128]{2,1,0:T(8,128)S(1)}, f32[1,32,128]{2,1,0:T(8,128)S(1)}) fusion(bf16[128,1024]{1,0:T(8,128)(2,1)S(1)} %collective-permute-done.2, bf16[128,1024]{1,0:T(8,128)(2,1)} %param.2, s32[]{:T(128)S(6)} %select_n.16), kind=kOutput, calls=%fused_computation.57 | convolution fusion | flops 8388607 | bytes 360452 | tf_op jit(solution)/shard_map/dot_general | solution.py:33
  49.5 1.0 %constant_dynamic-update-slice_fusion.5 = (f32[7,32,128]{2,1,0:T(8,128)S(1)}, f32[1,32,128]{2,1,0:T(8,128)S(1)}) fusion(f32[7,32,128]{2,1,0:T(8,128)S(1)} %get-tuple-element.5, bf16[128,1024]{1,0:T(8,128)(2,1)S(1)} %collective-permute-done.1, bf16[128,1024]{1,0:T(8,128)(2,1)} %param.2, s32[]{:T(128)S(6)} %select_n.16), kind=kOutput, calls=%fused_computation.56 | convolution fusion | flops 8388608 | bytes 360452 | tf_op jit(solution)/shard_map/dot_general | solution.py:33
  50.6 1.0 %constant_dynamic-update-slice_fusion.4 = (f32[7,32,128]{2,1,0:T(8,128)S(1)}, f32[1,32,128]{2,1,0:T(8,128)S(1)}) fusion(f32[7,32,128]{2,1,0:T(8,128)S(1)} %get-tuple-element.7, bf16[128,1024]{1,0:T(8,128)(2,1)S(1)} %collective-permute-done, bf16[128,1024]{1,0:T(8,128)(2,1)} %param.2, s32[]{:T(128)S(6)} %select_n.16), kind=kOutput, calls=%fused_computation.55 | convolution fusion | flops 8388608 | bytes 360452 | tf_op jit(solution)/shard_map/dot_general | solution.py:33
  51.6 1.2 %constant_dynamic-update-slice_fusion.3 = (f32[7,32,128]{2,1,0:T(8,128)S(1)}, f32[1,32,128]{2,1,0:T(8,128)S(1)}) fusion(f32[7,32,128]{2,1,0:T(8,128)S(1)} %get-tuple-element.9, bf16[128,1024]{1,0:T(8,128)(2,1)} %param.2, s32[]{:T(128)S(6)} %select_n.16), kind=kOutput, calls=%fused_computation.54 | convolution fusion | flops 8388608 | bytes 360452 | tf_op jit(solution)/shard_map/dot_general | solution.py:33
  52.8 0.7 fusion.22
  53.6 0.7 fusion.24
  54.3 0.7 fusion.26
  55.4 0.7 fusion.28
  56.3 2.5 %collective-permute-start.6 = (f32[7,32,128]{2,1,0:T(8,128)S(1)}, f32[7,32,128]{2,1,0:T(8,128)S(1)}, u32[]{:S(2)}, u32[]{:S(2)}) collective-permute-start(f32[7,32,128]{2,1,0:T(8,128)S(1)} %get-tuple-element.17), channel_id=1, source_target_pairs={{0,1},{1,2},{2,3},{3,0},{4,5},{5,6},{6,7},{7,4},{8,9},{9,10},{10,1... | collective-permute-start | bytes 344072 | tf_op jit(solution)/shard_map/ppermute | solution.py:20
  58.8 0.7 fusion.30
  59.5 4.0 %collective-permute-done.6 = f32[7,32,128]{2,1,0:T(8,128)S(1)} collective-permute-done((f32[7,32,128]{2,1,0:T(8,128)S(1)}, f32[7,32,128]{2,1,0:T(8,128)S(1)}, u32[]{:S(2)}, u32[]{:S(2)}) %collective-permute-start.6) | collective-permute-done | bytes 114720 | tf_op jit(solution)/shard_map/ppermute | solution.py:20
  63.5 0.8 %collective-permute-start.7 = (f32[7,32,128]{2,1,0:T(8,128)S(1)}, f32[7,32,128]{2,1,0:T(8,128)S(1)}, u32[]{:S(2)}, u32[]{:S(2)}) collective-permute-start(f32[7,32,128]{2,1,0:T(8,128)S(1)} %collective-permute-done.6), channel_id=1, source_target_pairs={{0,1},{1,2},{2,3},{3,0},{4,5},{5,6},{6,7},{7,4},{8,9},{9,10},{10,1... | collective-permute-start | bytes 344072 | tf_op jit(solution)/shard_map/ppermute | solution.py:20
  64.3 0.7 fusion.32
  65.0 4.3 %collective-permute-done.7 = f32[7,32,128]{2,1,0:T(8,128)S(1)} collective-permute-done((f32[7,32,128]{2,1,0:T(8,128)S(1)}, f32[7,32,128]{2,1,0:T(8,128)S(1)}, u32[]{:S(2)}, u32[]{:S(2)}) %collective-permute-start.7) | collective-permute-done | bytes 114720 | tf_op jit(solution)/shard_map/ppermute | solution.py:20
  69.4 0.7 fusion.34
  70.1 5.0 %collective-permute-done.8 = f32[7,32,128]{2,1,0:T(8,128)S(1)} collective-permute-done((f32[7,32,128]{2,1,0:T(8,128)S(1)}, f32[7,32,128]{2,1,0:T(8,128)S(1)}, u32[]{:S(2)}, u32[]{:S(2)}) %collective-permute-start.8) | collective-permute-done | bytes 114720 | tf_op jit(solution)/shard_map/ppermute | solution.py:20
  75.4 1.9 %multiply_convert_fusion.8 = bf16[7,8,128,128]{3,2,1,0:T(8,128)(2,1)} fusion(f32[7,8,128,128]{3,2,1,0:T(8,128)S(1)} %fusion.34, f32[7,128,128]{2,1,0:T(8,128)S(1)} %constant_dynamic-slice_fusion, f32[8]{0:T(128)S(1)} %broadcast_multiply_fusion), kind=kLoop, calls=%fused_computation.8 | loop fusion | flops 3670016 | bytes 5963808 | tf_op jit(solution)/shard_map/convert_element_type | solution.py:73
  (38 shorter events, 2.1 us)
Async XLA Ops:
  0.0 9.0 %collective-permute-start = (bf16[128,1024]{1,0:T(8,128)(2,1)}, bf16[128,1024]{1,0:T(8,128)(2,1)S(1)}, u32[]{:S(2)}, u32[]{:S(2)}) collective-permute-start(bf16[128,1024]{1,0:T(8,128)(2,1)} %param.2), channel_id=1, source_target_pairs={{28,0},{0,4},{4,8},{8,12},{12,16},{16,20},{20,24},{24,28},{29,1},{... | collective-permute-start | bytes 786440 | tf_op jit(solution)/shard_map/ppermute | solution.py:29
  0.5 9.2 %collective-permute-start.3 = (bf16[128,1024]{1,0:T(8,128)(2,1)}, bf16[128,1024]{1,0:T(8,128)(2,1)S(1)}, u32[]{:S(2)}, u32[]{:S(2)}) collective-permute-start(bf16[128,1024]{1,0:T(8,128)(2,1)} %param.2), channel_id=1, source_target_pairs={{4,0},{8,4},{12,8},{16,12},{20,16},{24,20},{28,24},{0,28},{5,1},{9... | collective-permute-start | bytes 786440 | tf_op jit(solution)/shard_map/ppermute | solution.py:29
  9.0 7.7 %collective-permute-start.1 = (bf16[128,1024]{1,0:T(8,128)(2,1)S(1)}, bf16[128,1024]{1,0:T(8,128)(2,1)S(1)}, u32[]{:S(2)}, u32[]{:S(2)}) collective-permute-start(bf16[128,1024]{1,0:T(8,128)(2,1)S(1)} %collective-permute-done), channel_id=1, source_target_pairs={{28,0},{0,4},{4,8},{8,12},{12,16},{16,20},{20,24},{24,28},{29,1},{... | collective-permute-start | bytes 786440 | tf_op jit(solution)/shard_map/ppermute | solution.py:29
  9.7 38.8 %collective-permute-start.4 = (bf16[128,1024]{1,0:T(8,128)(2,1)S(1)}, bf16[128,1024]{1,0:T(8,128)(2,1)S(1)}, u32[]{:S(2)}, u32[]{:S(2)}) collective-permute-start(bf16[128,1024]{1,0:T(8,128)(2,1)S(1)} %collective-permute-done.3), channel_id=1, source_target_pairs={{4,0},{8,4},{12,8},{16,12},{20,16},{24,20},{28,24},{0,28},{5,1},{9... | collective-permute-start | bytes 786440 | tf_op jit(solution)/shard_map/ppermute | solution.py:29
  16.7 31.8 %collective-permute-start.2 = (bf16[128,1024]{1,0:T(8,128)(2,1)S(1)}, bf16[128,1024]{1,0:T(8,128)(2,1)S(1)}, u32[]{:S(2)}, u32[]{:S(2)}) collective-permute-start(bf16[128,1024]{1,0:T(8,128)(2,1)S(1)} %collective-permute-done.1), channel_id=1, source_target_pairs={{28,0},{0,4},{4,8},{8,12},{12,16},{16,20},{20,24},{24,28},{29,1},{... | collective-permute-start | bytes 786440 | tf_op jit(solution)/shard_map/ppermute | solution.py:29
  48.4 7.7 %collective-permute-start.5 = (bf16[128,1024]{1,0:T(8,128)(2,1)S(1)}, bf16[128,1024]{1,0:T(8,128)(2,1)S(1)}, u32[]{:S(2)}, u32[]{:S(2)}) collective-permute-start(bf16[128,1024]{1,0:T(8,128)(2,1)S(1)} %collective-permute-done.4), channel_id=1, source_target_pairs={{4,0},{8,4},{12,8},{16,12},{20,16},{24,20},{28,24},{0,28},{5,1},{9... | collective-permute-start | bytes 786440 | tf_op jit(solution)/shard_map/ppermute | solution.py:29
  52.8 2.2 %copy-start = (bf16[128,1024]{1,0:T(8,128)(2,1)S(1)}, bf16[128,1024]{1,0:T(8,128)(2,1)}, u32[]{:S(2)}) copy-start(bf16[128,1024]{1,0:T(8,128)(2,1)} %param.2) | copy-start | bytes 786436
  56.3 7.2 %collective-permute-start.6 = (f32[7,32,128]{2,1,0:T(8,128)S(1)}, f32[7,32,128]{2,1,0:T(8,128)S(1)}, u32[]{:S(2)}, u32[]{:S(2)}) collective-permute-start(f32[7,32,128]{2,1,0:T(8,128)S(1)} %get-tuple-element.17), channel_id=1, source_target_pairs={{0,1},{1,2},{2,3},{3,0},{4,5},{5,6},{6,7},{7,4},{8,9},{9,10},{10,1... | collective-permute-start | bytes 344072 | tf_op jit(solution)/shard_map/ppermute | solution.py:20
  63.5 5.9 %collective-permute-start.7 = (f32[7,32,128]{2,1,0:T(8,128)S(1)}, f32[7,32,128]{2,1,0:T(8,128)S(1)}, u32[]{:S(2)}, u32[]{:S(2)}) collective-permute-start(f32[7,32,128]{2,1,0:T(8,128)S(1)} %collective-permute-done.6), channel_id=1, source_target_pairs={{0,1},{1,2},{2,3},{3,0},{4,5},{5,6},{6,7},{7,4},{8,9},{9,10},{10,1... | collective-permute-start | bytes 344072 | tf_op jit(solution)/shard_map/ppermute | solution.py:20
  69.4 5.7 %collective-permute-start.8 = (f32[7,32,128]{2,1,0:T(8,128)S(1)}, f32[7,32,128]{2,1,0:T(8,128)S(1)}, u32[]{:S(2)}, u32[]{:S(2)}) collective-permute-start(f32[7,32,128]{2,1,0:T(8,128)S(1)} %collective-permute-done.7), channel_id=1, source_target_pairs={{0,1},{1,2},{2,3},{3,0},{4,5},{5,6},{6,7},{7,4},{8,9},{9,10},{10,1... | collective-permute-start | bytes 344072 | tf_op jit(solution)/shard_map/ppermute | solution.py:20
